TPU v7x, 1024 devices: a whole 4x4x32 slice. The times are simulated.
1024 devices in a mesh: seq: 64 (over z, core), dp: 16 (over x, y).
Axes of the slice: x: 4, y: 4, z: 32, core: 2. Of those that a mesh axis runs over, the one named last changes fastest.
Arguments:
- queries: bfloat16 [16384, 8192], P('seq', 'dp'), may hold values from -6 to 6
- key_vectors: bfloat16 [16384, 8192], P('seq', 'dp'), may hold values from -6 to 6
- values: bfloat16 [16384, 8192], P('seq', 'dp'), may hold values from -6 to 6
- log_decay: float32 [64, 16384], P('dp', 'seq'), may hold values from -0.7 to 0, as said below
- norm_gain: float32 [8192], P('dp'), may hold values from 0.25 to 1.75
- grad_out: bfloat16 [16384, 8192], P('seq', 'dp'), may hold values from -16 to 16
Outputs:
- grad_queries: bfloat16 [16384, 8192], P('seq', 'dp')
- grad_keys: bfloat16 [16384, 8192], P('seq', 'dp')
- grad_values: bfloat16 [16384, 8192], P('seq', 'dp')
- grad_gain: float32 [8192], P('dp')
Inputs may be any that keep to these rules, and one draw needn't show every extreme that they name: `log_decay`: entries are negative.
All inputs are finite; a program needn't handle non-finite values.
Results may differ from a plain program's by a relative error of at most 0.0064.
Values sent between devices are 32-bit elements; how exact they have to be, the bound alone decides.
A program may use at most 64 MiB of HBM per device.

v0:
```python
import jax
import jax.numpy as jnp
from jax import lax
from jax.sharding import PartitionSpec as P

epsilon = 1e-06


def carried_in(part, axis, combine, identity, reverse):
    count = lax.axis_size(axis)
    place = lax.axis_index(axis)
    ahead = count - 1 - place if reverse else place
    gathered = jax.tree.map(lambda a: lax.all_gather(a, axis), part)
    state = jax.tree.map(lambda a, e: jnp.zeros_like(a) + jnp.asarray(e, a.dtype), part, identity)

    def one(lap, state):
        source = count - 1 - lap if reverse else lap
        return combine(
            state, jax.tree.map(lambda a: lax.dynamic_index_in_dim(a, source, 0, False), gathered)
        )

    return lax.fori_loop(0, ahead, one, state)


def combine(earlier_pair, later_pair):
    return (
        earlier_pair[0] + later_pair[0],
        jnp.exp(later_pair[0])[..., None, None] * earlier_pair[1] + later_pair[1],
    )


def block_terms(block_decay):
    position_index = block_decay.shape[2]
    running = jnp.cumsum(block_decay, axis=2)
    totals = running[:, :, -1]
    causal = lax.broadcasted_iota(
        jnp.int32, (position_index, position_index), 0
    ) >= lax.broadcasted_iota(jnp.int32, (position_index, position_index), 1)
    spread = running[:, :, :, None] - running[:, :, None, :]
    weights = jnp.where(causal, jnp.exp(jnp.where(causal, spread, 0.0)), 0.0)
    return (running, totals, weights)


def local(queries, key_vectors, values, log_decay, norm_gain, grad_out):
    position_index, row_width = queries.shape
    head_count = log_decay.shape[0]
    head_dim = row_width // head_count
    full_width = row_width * lax.axis_size("dp")
    shape_four = (1, position_index, head_count, head_dim)
    query_heads = queries.reshape(shape_four)
    key_heads = key_vectors.reshape(shape_four)
    value_heads = values.reshape(shape_four)
    running, totals, weights = block_terms(log_decay[None])
    growth = jnp.exp(running).transpose(0, 2, 1)[..., None]
    shrink = jnp.exp(totals[:, :, None] - running).transpose(0, 2, 1)[..., None]
    scores = jnp.einsum(
        "bthd,bshd->bhts", query_heads, key_heads, preferred_element_type=jnp.float32
    )
    score_low = (scores * weights).astype(jnp.bfloat16)
    query_scaled = (query_heads * growth).astype(jnp.bfloat16)
    key_scaled = (key_heads * shrink).astype(jnp.bfloat16)
    local_state = jnp.einsum(
        "bshd,bshe->bhde", key_scaled, value_heads, preferred_element_type=jnp.float32
    )
    inside = jnp.einsum(
        "bhts,bshe->bthe", score_low, value_heads, preferred_element_type=jnp.float32
    )
    identity = (jnp.zeros_like(totals), jnp.zeros_like(local_state))
    entering = carried_in((totals, local_state), "seq", combine, identity, False)
    state_low = entering[1].astype(jnp.bfloat16)
    attended = inside + jnp.einsum(
        "bthd,bhde->bthe", query_scaled, state_low, preferred_element_type=jnp.float32
    )
    square_sum = lax.psum(jnp.sum(attended * attended, axis=(2, 3), keepdims=True), "dp")
    norm_root = jnp.sqrt(square_sum / full_width + epsilon)
    normed = attended / norm_root
    gain_heads = norm_gain.reshape(head_count, head_dim)
    upstream = grad_out.reshape(shape_four)
    gain_part = jnp.sum(normed * upstream, axis=(0, 1)).reshape(row_width)
    grad_gain = lax.psum(gain_part, "seq")
    scaled = gain_heads * upstream
    projection = lax.psum(jnp.sum(scaled * normed, axis=(2, 3), keepdims=True), "dp")
    d_attended = ((scaled - normed * (projection / full_width)) / norm_root).astype(jnp.bfloat16)
    back_scores = jnp.einsum(
        "bthe,bshe->bhts", d_attended, value_heads, preferred_element_type=jnp.float32
    )
    grad_probs = (back_scores * weights).astype(jnp.bfloat16)
    out_scaled = (d_attended * growth).astype(jnp.bfloat16)
    value_scaled = (value_heads * shrink).astype(jnp.bfloat16)
    local_grad = jnp.einsum(
        "bthd,bthe->bhde", query_scaled, d_attended, preferred_element_type=jnp.float32
    )
    suffix = carried_in((totals, local_grad), "seq", combine, identity, True)
    later_low = suffix[1].astype(jnp.bfloat16)
    query_part = jnp.einsum(
        "bhts,bshd->bthd", grad_probs, key_heads, preferred_element_type=jnp.float32
    )
    query_part = query_part + jnp.einsum(
        "bthe,bhde->bthd", out_scaled, state_low, preferred_element_type=jnp.float32
    )
    key_part = jnp.einsum(
        "bhts,bthd->bshd", grad_probs, query_heads, preferred_element_type=jnp.float32
    )
    key_part = key_part + jnp.einsum(
        "bshe,bhde->bshd", value_scaled, later_low, preferred_element_type=jnp.float32
    )
    value_part = jnp.einsum(
        "bhts,bthe->bshe", score_low, d_attended, preferred_element_type=jnp.float32
    )
    value_part = value_part + jnp.einsum(
        "bshd,bhde->bshe", key_scaled, later_low, preferred_element_type=jnp.float32
    )
    flat_shape = (position_index, row_width)
    grad_queries = query_part.reshape(flat_shape).astype(jnp.bfloat16)
    grad_keys = key_part.reshape(flat_shape).astype(jnp.bfloat16)
    grad_values = value_part.reshape(flat_shape).astype(jnp.bfloat16)
    return (grad_queries, grad_keys, grad_values, grad_gain)


def solution(mesh):
    in_specs = (
        P("seq", "dp"),
        P("seq", "dp"),
        P("seq", "dp"),
        P("dp", "seq"),
        P("dp"),
        P("seq", "dp"),
    )
    out_specs = (P("seq", "dp"), P("seq", "dp"), P("seq", "dp"), P("dp"))
    return jax.shard_map(local, mesh=mesh, in_specs=in_specs, out_specs=out_specs, check_vma=False)
```

profile of v0, /device:TPU:1, one launch (start us, length us, event | category | flops | bytes accessed | tf_op | source)
XLA Modules:
  0.0 535.0 jit_solution(4968281636037175395)
XLA Ops:
  8.0 1.2 reduce-window.6
  9.7 2.2 fusion.16
  12.1 1.1 copy.108
  13.2 1.1 copy.68
  14.3 69.7 %all-gather = f32[64,4,1]{1,2,0:T(1,128)S(1)} all-gather(f32[1,4,1]{1,2,0:T(1,128)S(1)} %get-tuple-element.201), channel_id=2, replica_groups=mesh['seq'=64,'dp'=16] {'seq'}, dimensions={0}, use_global_device_ids=true | all-gather | bytes 1040 | tf_op jit(solution)/shard_map/all_gather | solution.py:13
  84.6 1.3 convolution_bitcast_fusion.2
  85.9 89.7 %all-gather.6.cloned.1.call-done = f32[256,128,128]{2,1,0:T(8,128)} async-done(((f32[4,128,128]{2,1,0:T(8,128)}), f32[256,128,128]{2,1,0:T(8,128)}) %all-gather.6.cloned.1.call-update) | async-done | bytes 16777232 | tf_op jit(solution)/shard_map/all_gather | solution.py:13
  175.5 1.1 while.26
  175.6 1.1 bitcast_add_fusion.7
  177.0 33.5 %psum.21 = f32[1,256,1,1]{1,3,2,0:T(1,128)S(1)} all-reduce(f32[1,256,1,1]{1,3,2,0:T(1,128)S(1)} %bitcast.190), channel_id=1, replica_groups=mesh['seq'=64,'dp'=16] {'dp'}, use_global_device_ids=true, to_apply=%region_5.6 | all-reduce | flops 256 | bytes 2048 | tf_op jit(solution)/shard_map/psum | solution.py:74
  211.4 28.8 %psum.22 = f32[1,256,1,1]{1,3,2,0:T(1,128)S(1)} all-reduce(f32[1,256,1,1]{1,3,2,0:T(1,128)S(1)} %bitcast.187), channel_id=1, replica_groups=mesh['seq'=64,'dp'=16] {'dp'}, use_global_device_ids=true, to_apply=%region_7.8 | all-reduce | flops 256 | bytes 2048 | tf_op jit(solution)/shard_map/psum | solution.py:82
  243.8 175.6 %psum.23 = f32[512]{0:T(512)} all-reduce(f32[512]{0:T(512)S(1)} %bitcast.186), channel_id=1, replica_groups=mesh['seq'=64,'dp'=16] {'seq'}, use_global_device_ids=true, to_apply=%region_11.12 | all-reduce | flops 512 | bytes 4096 | tf_op jit(solution)/shard_map/psum | solution.py:80
  419.9 37.3 %all-gather.8.cloned.1.call-done = f32[256,128,128]{2,1,0:T(8,128)} async-done(((f32[4,128,128]{2,1,0:T(8,128)}), f32[256,128,128]{2,1,0:T(8,128)}) %all-gather.8.cloned.1.call-update) | async-done | bytes 16777232 | tf_op jit(solution)/shard_map/all_gather | solution.py:13
  457.2 68.4 %while.27 = (s32[]{:T(128)}, f32[1,4,128,128]{3,2,1,0:T(8,128)S(1)}, s32[]{:T(128)}, f32[64,1,4]{2,1,0:T(1,128)S(1)}, f32[64,1,4,128,128]{4,3,2,1,0:T(8,128)}, /*index=5*/s32[]{:T(128)}, s32[]{:T(128)}, s32[]{:T(128)}, s32[]{:T(128)}) while((s32[]{:T(128)}, f32[1,4,128,128]{3,2,1,0:T(8,128)S(1)}, s32[]{:T(128)}, f32[64,1,4]{2,1,0:T(1,128)S(1)}, ...), condition=%wide.region_9.10_spmd, body=%wide.region_8.9_spmd.sunk | while | flops 131078 | bytes 786635 | solution.py:22
  458.4 1.1 bitcast_add_fusion.8
  459.5 1.1 bitcast_add_fusion.8
  460.6 1.1 bitcast_add_fusion.8
  461.7 1.1 bitcast_add_fusion.8
  462.8 1.1 bitcast_add_fusion.8
  463.9 1.1 bitcast_add_fusion.8
  469.4 1.1 bitcast_add_fusion.8
  470.5 1.1 bitcast_add_fusion.8
  471.6 1.1 bitcast_add_fusion.8
  472.7 1.1 bitcast_add_fusion.8
  473.8 1.1 bitcast_add_fusion.8
  474.9 1.1 bitcast_add_fusion.8
  479.3 1.1 bitcast_add_fusion.8
  480.4 1.1 bitcast_add_fusion.8
  481.5 1.1 bitcast_add_fusion.8
  482.6 1.1 bitcast_add_fusion.8
  483.7 1.1 bitcast_add_fusion.8
  484.8 1.1 bitcast_add_fusion.8
  490.4 1.1 bitcast_add_fusion.8
  491.5 1.1 bitcast_add_fusion.8
  492.6 1.1 bitcast_add_fusion.8
  493.7 1.1 bitcast_add_fusion.8
  494.8 1.1 bitcast_add_fusion.8
  495.9 1.1 bitcast_add_fusion.8
  500.3 1.1 bitcast_add_fusion.8
  501.4 1.1 bitcast_add_fusion.8
  502.5 1.1 bitcast_add_fusion.8
  503.6 1.1 bitcast_add_fusion.8
  504.7 1.1 bitcast_add_fusion.8
  505.8 1.1 bitcast_add_fusion.8
  511.3 1.1 bitcast_add_fusion.8
  512.4 1.1 bitcast_add_fusion.8
  513.5 1.1 bitcast_add_fusion.8
  514.6 1.1 bitcast_add_fusion.8
  (133 shorter events, 40.3 us)
Async XLA Ops:
  7.2 2.6 copy-start
  7.2 234.7 %copy-start.1 = (bf16[256,512]{1,0:T(8,128)(2,1)S(1)}, bf16[256,512]{1,0:T(8,128)(2,1)}, u32[]{:S(2)}) copy-start(bf16[256,512]{1,0:T(8,128)(2,1)} %param.12) | copy-start | bytes 786436
  7.2 168.3 %all-gather.6.cloned.1.call-start = ((), (), s32[]{:S(2)}) async-start(), calls=%async_computation | async-start | bytes 17039360 | tf_op jit(solution)/shard_map/all_gather | solution.py:13
  11.9 445.3 %all-gather.8.cloned.1.call-start = ((), (), s32[]{:S(2)}) async-start(), calls=%async_computation.1 | async-start | bytes 17039360 | tf_op jit(solution)/shard_map/all_gather | solution.py:13
Sparse Core Ops, SparseCore 0:
  12.0 163.4 all-gather.5
  242.0 215.1 all-gather.7
where the time goes:
time: 537 us; the launch traced here: 535 us
  blocking collectives  308 us (57%)
  waiting for transfers between devices  127 us (24%)
  other arithmetic  69.9 us (13%)
  between operations  14.2 us (3%)
  matrix products  7.39 us (1%)
  local copies, waits for them, and re-layouts  6.8 us (1%)
    psum x1, blocking collectives, local(): grad_gain = lax.psum(gain_part, 'seq')  176 us
    all_gather x2, waiting for transfers between devices, carried_in(): gathered = jax.tree.map(lambda a: lax.all_gather(a, axis), part)  127 us
    all_gather x1, blocking collectives, carried_in(): gathered = jax.tree.map(lambda a: lax.all_gather(a, axis), part)  69.7 us
    add x63, other arithmetic, combine(): jnp.exp(later_pair[0])[..., None, None] * earlier_pair[1] + later_pair[1]  66.8 us
    psum x1, blocking collectives, local(): lax.psum(jnp.sum(attended * attended, axis=(2, 3), keepdims=True), 'dp')  33.5 us
    psum x1, blocking collectives, local(): lax.psum(jnp.sum(scaled * normed, axis=(2, 3), keepdims=True), 'dp')  28.8 us
  transfers between devices with their start and end apart: 2, of which 2 were waited for; matrix products, arithmetic and copies ran while one was open for 1% of the time, Pallas kernels for 0%

commit v1 on v0

v1 whole, which is shorter than its diff:
```python
import functools

import jax
import jax.numpy as jnp
from jax import lax
from jax.experimental import pallas as pl
from jax.experimental.pallas import tpu as pltpu
from jax.sharding import PartitionSpec as P

epsilon = 1e-06
f32 = jnp.float32
bf16 = jnp.bfloat16
MESH = pl.DeviceIdType.MESH

NN = (((1,), (0,)), ((), ()))
NT = (((1,), (1,)), ((), ()))
TN = (((0,), (0,)), ((), ()))


def mm(a, b, dims):
    return lax.dot_general(a, b, dims, preferred_element_type=f32)


def kernel(
    cores,
    q_ref, k_ref, v_ref, ld_ref, gain_ref, go_ref,
    gq_ref, gk_ref, gv_ref, gg_ref,
    eg, eg_sib, w_buf, p_buf, qs_buf, ks_buf, in_buf, d_buf, s_low, r_low,
    growth_buf, shrink_buf, dp_send, dp_recv, gain_own, gain_sib, gain_chip, gain_recv, gain_out,
    state, half_recv, t_send, t_recv, e_send, e_recv, x_send, x_recv,
    dec_send, dec_recv,
    send_sem, recv_sem,
):
    seq = lax.axis_size("seq")
    dps = lax.axis_size("dp")
    chips = seq // cores
    place = lax.axis_index("seq")
    row = lax.axis_index("dp")
    z = lax.div(place, cores)
    core = lax.rem(place, cores)
    sibling = place + 1 - 2 * core
    positions, width = q_ref.shape
    heads = ld_ref.shape[0]
    dim = width // heads
    half = heads // 2
    slab = half * dim // chips

    def chip_peer(step):
        return lax.rem(z + step, chips) * cores + core

    barrier = pltpu.get_barrier_semaphore()
    pl.semaphore_signal(barrier, inc=1, device_id={"seq": sibling}, device_id_type=MESH)

    def greet_chip(step, carry):
        pl.semaphore_signal(
            barrier, inc=1, device_id={"seq": chip_peer(step)}, device_id_type=MESH
        )
        return carry

    def greet_row(step, carry):
        pl.semaphore_signal(
            barrier, inc=1, device_id={"dp": lax.rem(row + step, dps)}, device_id_type=MESH
        )
        return carry

    lax.fori_loop(1, chips, greet_chip, 0)
    lax.fori_loop(1, dps, greet_row, 0)

    ld = ld_ref[...]
    run = jnp.concatenate([ld, ld], axis=0)
    lane = lax.broadcasted_iota(jnp.int32, run.shape, 1)
    step = 1
    while step < positions:
        run = run + jnp.where(lane >= step, pltpu.roll(run, step, 1), 0.0)
        step *= 2

    def columns(line):
        return jnp.transpose(jnp.broadcast_to(line, (dim, positions)))

    for h in range(heads):
        line = run[h : h + 1]
        last = run[h : h + 1, positions - 1 : positions]
        eg[h] = jnp.broadcast_to(jnp.exp(last), (1, dim))
        span = slice(h * dim, (h + 1) * dim)
        column = columns(line)
        shrink = jnp.exp(last - column)
        shrink_buf[h] = shrink
        growth_buf[h] = jnp.exp(column)
        key_scaled = (k_ref[:, span].astype(f32) * shrink).astype(bf16)
        ks_buf[h] = key_scaled
        state[0, h] = mm(key_scaled, v_ref[:, span], TN)

    def inner_forward():
        causal = lax.broadcasted_iota(
            jnp.int32, (positions, positions), 0
        ) >= lax.broadcasted_iota(jnp.int32, (positions, positions), 1)
        for h in range(heads):
            span = slice(h * dim, (h + 1) * dim)
            line = run[h : h + 1]
            column = columns(line)
            wide = jnp.concatenate([column] * (positions // dim), axis=1)
            spread = jnp.where(causal, wide - line, 0.0)
            weights = jnp.where(causal, jnp.exp(spread), 0.0)
            w_buf[h] = weights
            q = q_ref[:, span]
            probs = (mm(q, k_ref[:, span], NT) * weights).astype(bf16)
            p_buf[h] = probs
            qs_buf[h] = (q.astype(f32) * growth_buf[h]).astype(bf16)
            in_buf[h] = mm(probs, v_ref[:, span], NN)

    inner_forward()

    pl.semaphore_wait(barrier, chips + dps - 1)

    def copy(src, dst, index, target):
        return pltpu.make_async_remote_copy(
            src_ref=src,
            dst_ref=dst,
            send_sem=send_sem.at[index],
            recv_sem=recv_sem.at[index],
            device_id=target,
            device_id_type=MESH,
        )

    def spread_out(make):
        make(chips // 2).start()

        def one(t, carry):
            make(chips // 2 - t).start()
            make(chips // 2 + t).start()
            return carry

        lax.fori_loop(1, chips // 2, one, 0)

    mine = pl.ds(core * half, half)
    other = pl.ds((1 - core) * half, half)

    def scan(turn, low, fill, gain_too):
        base = turn * 8
        late = core if turn == 0 else 1 - core
        early = late == 0
        swap = copy(state.at[turn, other], half_recv.at[turn], base, {"seq": sibling})
        swap.start()
        if turn == 0:
            tell = copy(eg, eg_sib, base + 1, {"seq": sibling})
            tell.start()
            tell.wait()
        if gain_too:
            share = copy(gain_own.at[other], gain_sib, base + 1, {"seq": sibling})
            share.start()
        swap.wait()
        own = state[turn, mine]
        theirs = half_recv[turn]
        decay_own = eg[mine]
        decay_sib = eg_sib[mine]
        total = jnp.where(early, decay_sib, 1.0) * own + jnp.where(early, 1.0, decay_own) * theirs
        t_send[turn] = total.reshape(chips, slab, dim)
        if turn == 0:
            chip_decay = decay_own * decay_sib
            for c in range(chips):
                dec_send[c] = chip_decay[c * slab // dim]

        def give(step):
            peer = lax.rem(z + step, chips)
            return copy(
                t_send.at[turn, peer], t_recv.at[turn, z], base + 2, {"seq": peer * cores + core}
            )

        def give_decay(step):
            peer = lax.rem(z + step, chips)
            return copy(dec_send.at[peer], dec_recv.at[z], base + 3, {"seq": peer * cores + core})

        spread_out(give)
        if turn == 0:
            spread_out(give_decay)
        if gain_too:
            share.wait()
            gain_chip[...] = gain_own[mine] + gain_sib[...]

            def give_gain(step):
                peer = lax.rem(z + step, chips)
                return copy(gain_chip, gain_recv.at[z], base + 3, {"seq": peer * cores + core})

            spread_out(give_gain)
        fill()
        rest = pl.ds(0, chips - 1)
        copy(t_send.at[turn, rest], t_recv.at[turn, rest], base + 2, {"seq": sibling}).wait()
        if turn == 0:
            copy(dec_send.at[rest], dec_recv.at[rest], base + 3, {"seq": sibling}).wait()
            dec_recv[z] = dec_send[z]
        t_recv[turn, z] = t_send[turn, z]

        def advance(t, carry):
            i = t if turn == 0 else chips - 1 - t
            e_send[turn, i] = carry
            return dec_recv[i] * carry + t_recv[turn, i]

        lax.fori_loop(0, chips, advance, jnp.zeros((slab, dim), f32))

        def hand_back(step):
            peer = lax.rem(z + step, chips)
            return copy(
                e_send.at[turn, peer], e_recv.at[turn, z], base + 4, {"seq": peer * cores + core}
            )

        spread_out(hand_back)
        if gain_too:
            copy(gain_recv.at[rest], gain_recv.at[rest], base + 3, {"seq": sibling}).wait()
            gain_recv[z] = gain_chip[...]
            gain_out[mine] = jnp.sum(gain_recv[...], axis=0)
            trade = copy(gain_out.at[mine], gain_out.at[mine], base + 5, {"seq": sibling})
            trade.start()
        copy(e_send.at[turn, rest], e_recv.at[turn, rest], base + 4, {"seq": sibling}).wait()
        e_recv[turn, z] = e_send[turn, z]
        entering = e_recv[turn].reshape(half, dim, dim)
        x_send[turn] = jnp.where(early, decay_own, 1.0) * entering + jnp.where(early, 1.0, 0.0) * own
        pass_on = copy(x_send.at[turn], x_recv.at[turn], base + 6, {"seq": sibling})
        pass_on.start()
        kept = jnp.where(early, 1.0, decay_sib) * entering + jnp.where(early, 0.0, 1.0) * theirs
        low[mine] = kept.astype(bf16)
        pass_on.wait()
        low[other] = x_recv[turn].astype(bf16)
        if gain_too:
            trade.wait()

    scan(0, s_low, lambda: None, False)

    squares = jnp.zeros((positions, dim), f32)
    products = jnp.zeros((positions, dim), f32)
    for h in range(heads):
        span = slice(h * dim, (h + 1) * dim)
        attended = in_buf[h] + mm(qs_buf[h], s_low[h], NN)
        in_buf[h] = attended
        squares = squares + attended * attended
        scaled = gain_ref[:, span] * go_ref[:, span].astype(f32)
        products = products + scaled * attended
    dp_send[0:1] = jnp.sum(jnp.transpose(squares), axis=0, keepdims=True)
    dp_send[1:2] = jnp.sum(jnp.transpose(products), axis=0, keepdims=True)

    def to_row(step, carry):
        peer = lax.rem(row + step, dps)
        copy(dp_send, dp_recv.at[row], 16, {"dp": peer}).start()
        return carry

    lax.fori_loop(1, dps, to_row, 0)
    others = pl.ds(0, dps - 1)
    copy(dp_recv.at[others], dp_recv.at[others], 16, {"seq": sibling}).wait()
    dp_recv[row] = dp_send[...]
    sums = jnp.sum(dp_recv[...], axis=0)
    full = width * dps
    inverse = 1.0 / jnp.sqrt(sums[0:1] / full + epsilon)
    mean = sums[1:2] * inverse / full
    inverse_column = columns(inverse)
    mean_column = columns(mean)
    for h in range(heads):
        span = slice(h * dim, (h + 1) * dim)
        upstream = go_ref[:, span].astype(f32)
        normed = in_buf[h] * inverse_column
        gain_own[h] = jnp.sum(normed * upstream, axis=0, keepdims=True)
        scaled = gain_ref[:, span] * upstream
        d_low = ((scaled - normed * mean_column) * inverse_column).astype(bf16)
        d_buf[h] = d_low
        state[1, h] = mm(qs_buf[h], d_low, TN)

    def inner_backward():
        for h in range(heads):
            span = slice(h * dim, (h + 1) * dim)
            d_low = d_buf[h]
            grad_probs = (mm(d_low, v_ref[:, span], NT) * w_buf[h]).astype(bf16)
            out_scaled = (d_low.astype(f32) * growth_buf[h]).astype(bf16)
            gq = mm(grad_probs, k_ref[:, span], NN) + mm(out_scaled, s_low[h], NT)
            gq_ref[:, span] = gq.astype(bf16)
            in_buf[h] = mm(grad_probs, q_ref[:, span], TN)
            growth_buf[h] = mm(p_buf[h], d_low, TN)

    scan(1, r_low, inner_backward, True)

    for h in range(heads):
        span = slice(h * dim, (h + 1) * dim)
        value_scaled = (v_ref[:, span].astype(f32) * shrink_buf[h]).astype(bf16)
        gk = in_buf[h] + mm(value_scaled, r_low[h], NT)
        gk_ref[:, span] = gk.astype(bf16)
        gv = growth_buf[h] + mm(ks_buf[h], r_low[h], NN)
        gv_ref[:, span] = gv.astype(bf16)
        gg_ref[:, span] = gain_out[h]


def local(cores, queries, key_vectors, values, log_decay, norm_gain, grad_out):
    positions, width = queries.shape
    heads = log_decay.shape[0]
    dim = width // heads
    half = heads // 2
    chips = lax.axis_size("seq") // cores
    dps = lax.axis_size("dp")
    slab = half * dim // chips
    vmem = pl.BlockSpec(memory_space=pltpu.VMEM)
    grad = jax.ShapeDtypeStruct((positions, width), bf16)
    scratch = [
        pltpu.VMEM((heads, 1, dim), f32),
        pltpu.VMEM((heads, 1, dim), f32),
        pltpu.VMEM((heads, positions, positions), f32),
        pltpu.VMEM((heads, positions, positions), bf16),
        pltpu.VMEM((heads, positions, dim), bf16),
        pltpu.VMEM((heads, positions, dim), bf16),
        pltpu.VMEM((heads, positions, dim), f32),
        pltpu.VMEM((heads, positions, dim), bf16),
        pltpu.VMEM((heads, dim, dim), bf16),
        pltpu.VMEM((heads, dim, dim), bf16),
        pltpu.VMEM((heads, positions, dim), f32),
        pltpu.VMEM((heads, positions, dim), f32),
        pltpu.VMEM((2, positions), f32),
        pltpu.VMEM((dps, 2, positions), f32),
        pltpu.VMEM((heads, 1, dim), f32),
        pltpu.VMEM((half, 1, dim), f32),
        pltpu.VMEM((half, 1, dim), f32),
        pltpu.VMEM((chips, half, 1, dim), f32),
        pltpu.VMEM((heads, 1, dim), f32),
        pltpu.VMEM((2, heads, dim, dim), f32),
        pltpu.VMEM((2, half, dim, dim), f32),
        pltpu.VMEM((2, chips, slab, dim), f32),
        pltpu.VMEM((2, chips, slab, dim), f32),
        pltpu.VMEM((2, chips, slab, dim), f32),
        pltpu.VMEM((2, chips, slab, dim), f32),
        pltpu.VMEM((2, half, dim, dim), f32),
        pltpu.VMEM((2, half, dim, dim), f32),
        pltpu.VMEM((chips, 1, dim), f32),
        pltpu.VMEM((chips, 1, dim), f32),
        pltpu.SemaphoreType.DMA((17,)),
        pltpu.SemaphoreType.DMA((17,)),
    ]
    gq, gk, gv, gg = pl.pallas_call(
        functools.partial(kernel, cores),
        out_shape=(grad, grad, grad, jax.ShapeDtypeStruct((1, width), f32)),
        in_specs=[vmem] * 6,
        out_specs=(vmem, vmem, vmem, vmem),
        scratch_shapes=scratch,
        compiler_params=pltpu.CompilerParams(
            collective_id=0, has_side_effects=True, vmem_limit_bytes=48 * 1024 * 1024
        ),
    )(queries, key_vectors, values, log_decay, norm_gain.reshape(1, width), grad_out)
    return gq, gk, gv, gg.reshape(width)


def solution(mesh):
    in_specs = (
        P("seq", "dp"),
        P("seq", "dp"),
        P("seq", "dp"),
        P("dp", "seq"),
        P("dp"),
        P("seq", "dp"),
    )
    out_specs = (P("seq", "dp"), P("seq", "dp"), P("seq", "dp"), P("dp"))
    body = functools.partial(local, 2)
    return jax.shard_map(body, mesh=mesh, in_specs=in_specs, out_specs=out_specs, check_vma=False)
```

time: 537 us -> 122 us (0.23)
  blocking collectives: 308 us -> 0 us
  waiting for transfers between devices: 127 us -> 0 us
  Pallas kernels: 0 us -> 113 us
  other arithmetic: 69.9 us -> 0 us
  between operations: 14.2 us -> 0.66 us
  matrix products: 7.39 us -> 0 us
    psum x3 -> x0, blocking collectives: 238 us -> none  [the longest x1 176 us: local(): grad_gain = lax.psum(gain_part, 'seq')]
    all_gather x2 -> x0, waiting for transfers between devices: 127 us -> none  [carried_in(): gathered = jax.tree.map(lambda a: lax.all_gather(a, axis), part)]
    pallas_call x0 -> x1, Pallas kernels: none -> 113 us  [local(): pl.pallas_call(functools.partial(kernel, cores), out_shape=(grad, grad, g...]
    all_gather x1 -> x0, blocking collectives: 69.7 us -> none  [carried_in(): gathered = jax.tree.map(lambda a: lax.all_gather(a, axis), part)]
    add x63 -> x0, other arithmetic: 66.8 us -> none  [combine(): jnp.exp(later_pair[0])[..., None, None] * earlier_pair[1] + later_pair[1]]
    dot_general x12 -> x0, matrix products: 7.39 us -> none  [the longest x1 2.17 us: local(): jnp.einsum('bshd,bshe->bhde', key_scaled, value_heads, preferred_element_...]
  transfers between devices with their start and end apart: 2 -> 0, of which waited for: 2 -> 0; matrix products, arithmetic and copies ran while one was open for 1% -> 0% of each run, Pallas kernels for 0% -> 0%
where the time goes in v1:
time: 122 us; the launch traced here: 121 us
  Pallas kernels  113 us (93%)
  local copies, waits for them, and re-layouts  7.85 us (6%)
    pallas_call x1, Pallas kernels, local(): pl.pallas_call(functools.partial(kernel, cores), out_shape=(grad, grad, g...  113 us
    unnamed x16, local copies, waits for them, and re-layouts  7.85 us

profile of v1, /device:TPU:1, one launch (start us, length us, event | category | flops | bytes accessed | tf_op | source)
XLA Modules:
  0.0 121.4 jit_solution(12083091918359000662)
XLA Ops:
  0.6 0.0 copy-start
  0.6 0.9 copy-done
  1.6 0.0 copy-start.1
  1.6 0.9 copy-done.1
  2.5 0.0 copy-start.2
  2.5 0.9 copy-done.2
  3.5 0.0 copy-start.3
  3.5 0.9 copy-done.3
  4.4 0.0 copy-start.4
  4.4 0.7 copy-done.4
  5.1 0.0 copy-start.5
  5.1 0.7 copy-done.5
  5.8 112.9 %shard_map.93 = (bf16[256,512]{1,0:T(8,128)(2,1)S(1)}, bf16[256,512]{1,0:T(8,128)(2,1)S(1)}, bf16[256,512]{1,0:T(8,128)(2,1)S(1)}, f32[1,512]{1,0:T(1,128)S(1)}) custom-call(bf16[256,512]{1,0:T(8,128)(2,1)S(1)} %copy-done, bf16[256,512]{1,0:T(8,128)(2,1)S(1)} %copy-done.1, bf16[256,512]{1,0:T(8,128)(2,1)S(1)} %copy-done.2, f32[4,256]{1,0:T(4,128)S(1)} %copy-done.4, ...), custom_call_target="tpu_custom_call" | custom-call | tf_op jit(solution)/shard_map/pallas_call | solution.py:331
  118.7 0.7 copy.14
  119.4 0.7 copy.15
  120.1 0.7 copy.16
  120.8 0.6 copy.17
Async XLA Ops:
  0.6 1.0 copy-start
  1.6 0.9 copy-start.1
  2.5 0.9 copy-start.2
  3.5 0.9 copy-start.3
  4.4 0.7 copy-start.4
  5.1 0.7 copy-start.5

commit v2 on v1

v2 whole, which is shorter than its diff:
```python
import functools

import jax
import jax.numpy as jnp
from jax import lax
from jax.experimental import pallas as pl
from jax.experimental.pallas import tpu as pltpu
from jax.sharding import PartitionSpec as P

epsilon = 1e-06
f32 = jnp.float32
bf16 = jnp.bfloat16
MESH = pl.DeviceIdType.MESH

NN = (((1,), (0,)), ((), ()))
NT = (((1,), (1,)), ((), ()))
TN = (((0,), (0,)), ((), ()))

GROUP, ALL, BACK, MEMBERS, ROW = 0, 1, 2, 3, 8


def mm(a, b, dims):
    return lax.dot_general(a, b, dims, preferred_element_type=f32)


def exchange_kernel(
    q_hbm, k_hbm, v_hbm, ld_hbm, gain_hbm, go_hbm,
    gq_ref, gk_part, gv_part, vs_ref, ks_ref, r_low, gg_ref,
    q_ref, k_ref, v_ref, ld_ref, gain_ref, go_ref, load_sem,
    w_buf, p_buf, qs_buf, in_buf, d_buf, s_low, growth_buf,
    dp_send, dp_recv,
    state, part, all_send, all_recv, back_send, back_recv, member_send, member_recv,
    send_sem, recv_sem,
):
    seq = lax.axis_size("seq")
    dps = lax.axis_size("dp")
    place = lax.axis_index("seq")
    row = lax.axis_index("dp")
    positions, width = q_ref.shape
    heads = ld_ref.shape[0]
    dim = width // heads
    groups = seq // heads
    group = lax.div(place, heads)
    member = lax.rem(place, heads)
    slices = groups // 2
    slab = dim // slices
    ahead = slices // 2
    behind = slices - 1 - ahead

    loads = [
        pltpu.make_async_copy(src, dst, load_sem.at[i])
        for i, (src, dst) in enumerate(
            (
                (ld_hbm, ld_ref),
                (k_hbm, k_ref),
                (v_hbm, v_ref),
                (q_hbm, q_ref),
                (go_hbm, go_ref),
                (gain_hbm, gain_ref),
            )
        )
    ]
    for load in loads:
        load.start()

    def in_group(step):
        return group * heads + lax.rem(member + step, heads)

    def in_all(step):
        return lax.rem(group + step, groups) * heads + member

    barrier = pltpu.get_barrier_semaphore()

    def greet(target):
        pl.semaphore_signal(barrier, inc=1, device_id=target, device_id_type=MESH)

    def greet_all(step, carry):
        greet({"seq": in_all(step)})
        return carry

    def greet_row(step, carry):
        greet({"dp": lax.rem(row + step, dps)})
        return carry

    lax.fori_loop(1, groups, greet_all, 0)
    lax.fori_loop(1, dps, greet_row, 0)
    for step in range(1, heads):
        greet({"seq": in_group(step)})

    loads[0].wait()
    ld = ld_ref[...]
    run = jnp.concatenate([ld, ld], axis=0)
    lane = lax.broadcasted_iota(jnp.int32, run.shape, 1)
    step = 1
    while step < positions:
        run = run + jnp.where(lane >= step, pltpu.roll(run, step, 1), 0.0)
        step *= 2

    def columns(line):
        return jnp.transpose(jnp.broadcast_to(line, (dim, positions)))

    loads[1].wait()
    loads[2].wait()
    for h in range(heads):
        last = run[h : h + 1, positions - 1 : positions]
        span = slice(h * dim, (h + 1) * dim)
        column = columns(run[h : h + 1])
        shrink = jnp.exp(last - column)
        growth_buf[h] = jnp.exp(column)
        v = v_ref[:, span]
        key_scaled = (k_ref[:, span].astype(f32) * shrink).astype(bf16)
        ks_ref[h] = key_scaled
        vs_ref[h] = (v.astype(f32) * shrink).astype(bf16)
        state[0, h, 0:dim] = mm(key_scaled, v, TN)
        state[0, h, dim : dim + 1] = jnp.broadcast_to(jnp.exp(last), (1, dim))

    loads[3].wait()
    causal = lax.broadcasted_iota(
        jnp.int32, (positions, positions), 0
    ) >= lax.broadcasted_iota(jnp.int32, (positions, positions), 1)
    for h in range(heads):
        span = slice(h * dim, (h + 1) * dim)
        line = run[h : h + 1]
        wide = jnp.concatenate([columns(line)] * (positions // dim), axis=1)
        spread = jnp.where(causal, wide - line, 0.0)
        weights = jnp.where(causal, jnp.exp(spread), 0.0)
        w_buf[h] = weights
        q = q_ref[:, span]
        probs = (mm(q, k_ref[:, span], NT) * weights).astype(bf16)
        p_buf[h] = probs
        qs_buf[h] = (q.astype(f32) * growth_buf[h]).astype(bf16)
        in_buf[h] = mm(probs, v_ref[:, span], NN)
    loads[4].wait()
    loads[5].wait()

    pl.semaphore_wait(barrier, groups - 1 + dps - 1 + heads - 1)

    def copy(src, dst, index, target):
        return pltpu.make_async_remote_copy(
            src_ref=src,
            dst_ref=dst,
            send_sem=send_sem.at[index],
            recv_sem=recv_sem.at[index],
            device_id=target,
            device_id_type=MESH,
        )

    neighbour = {"seq": in_group(1)}

    def give_head(turn, h):
        rows = pl.ds(0, dim + 1)

        @pl.when(h != member)
        def _():
            copy(
                state.at[turn, h, rows],
                part.at[turn, member, rows],
                turn * 4 + GROUP,
                {"seq": group * heads + h},
            ).start()

    def whole_group(turn):
        box = part.at[turn, pl.ds(0, heads - 1), pl.ds(0, dim + 1)]
        return copy(box, box, turn * 4 + GROUP, neighbour)

    def whole_all(turn):
        box = all_recv.at[turn, pl.ds(0, groups - 1)]
        return copy(box, box, turn * 4 + ALL, neighbour)

    def whole_back(turn):
        box = back_recv.at[turn, pl.ds(0, slices - 1)]
        return copy(box, box, turn * 4 + BACK, neighbour)

    def whole_members(turn):
        rows = dim + turn
        box = member_recv.at[turn, pl.ds(0, heads - 1), pl.ds(0, rows)]
        return copy(box, box, turn * 4 + MEMBERS, neighbour)

    def whole_row():
        box = dp_recv.at[pl.ds(0, dps - 1)]
        return copy(box, box, ROW, neighbour)

    def scan(turn, fill):
        order = range(heads) if turn == 0 else range(heads - 1, -1, -1)
        whole_group(turn).wait_recv()
        part[turn, member] = state[turn, member]
        decay = [part[0, i, dim : dim + 1] for i in range(heads)]
        total = None
        for i in order:
            own = part[turn, i, 0:dim]
            total = own if total is None else decay[i] * total + own
        if turn == 0:
            tail = decay[0]
            for i in range(1, heads):
                tail = tail * decay[i]
        else:
            tail = part[1, 0, dim : dim + 1]
            for i in range(1, heads):
                tail = tail + part[1, i, dim : dim + 1]
        for s in range(slices):
            all_send[turn, s, 0:slab] = total[s * slab : (s + 1) * slab]
            all_send[turn, s, slab : slab + 1] = tail

        def give(step):
            target = lax.rem(group + step, groups)
            copy(
                all_send.at[turn, lax.rem(target, slices)],
                all_recv.at[turn, group],
                turn * 4 + ALL,
                {"seq": target * heads + member},
            ).start()

        give(slices)

        def both(t, carry):
            give(slices - t)
            give(slices + t)
            return carry

        lax.fori_loop(1, slices, both, 0)
        fill()
        whole_all(turn).wait_recv()
        all_recv[turn, group] = all_send[turn, lax.rem(group, slices)]
        carry = jnp.zeros((slab, dim), f32)
        for i in range(groups) if turn == 0 else range(groups - 1, -1, -1):
            back_send[turn, i] = carry
            carry = all_recv[0, i, slab : slab + 1] * carry + all_recv[turn, i, 0:slab]

        def give_back(step):
            target = lax.rem(group + groups + step, groups)
            copy(
                back_send.at[turn, target],
                back_recv.at[turn, lax.rem(group, slices)],
                turn * 4 + BACK,
                {"seq": target * heads + member},
            ).start()

        for t in range(ahead, 0, -1):
            give_back(t)
            if t <= behind:
                give_back(-t)
        if turn == 1:
            gain_total = all_recv[1, 0, slab : slab + 1]
            for i in range(1, groups):
                gain_total = gain_total + all_recv[1, i, slab : slab + 1]
        if slices > 1:
            whole_back(turn).wait_recv()
        back_recv[turn, lax.rem(group, slices)] = back_send[turn, group]
        entering = back_recv[turn].reshape(dim, dim)
        for i in order:
            member_send[turn, i, 0:dim] = entering
            entering = decay[i] * entering + part[turn, i, 0:dim]
            if turn == 1:
                member_send[turn, i, dim : dim + 1] = gain_total
        rows = pl.ds(0, dim + turn)
        for t in (2, 1, 3) if heads == 4 else range(1, heads):
            target = lax.rem(member + t, heads)
            copy(
                member_send.at[turn, target, rows],
                member_recv.at[turn, member, rows],
                turn * 4 + MEMBERS,
                {"seq": group * heads + target},
            ).start()
        whole_members(turn).wait_recv()
        member_recv[turn, member] = member_send[turn, member]

    for h in range(heads):
        give_head(0, h)
    scan(0, lambda: None)

    squares = jnp.zeros((positions, dim), f32)
    products = jnp.zeros((positions, dim), f32)
    for h in range(heads):
        span = slice(h * dim, (h + 1) * dim)
        low = member_recv[0, h, 0:dim].astype(bf16)
        s_low[h] = low
        attended = in_buf[h] + mm(qs_buf[h], low, NN)
        in_buf[h] = attended
        squares = squares + attended * attended
        scaled = gain_ref[:, span] * go_ref[:, span].astype(f32)
        products = products + scaled * attended
    dp_send[0:1] = jnp.sum(jnp.transpose(squares), axis=0, keepdims=True)
    dp_send[1:2] = jnp.sum(jnp.transpose(products), axis=0, keepdims=True)

    def to_row(step, carry):
        copy(dp_send, dp_recv.at[row], ROW, {"dp": lax.rem(row + step, dps)}).start()
        return carry

    lax.fori_loop(1, dps, to_row, 0)
    if dps > 1:
        whole_row().wait_recv()
    dp_recv[row] = dp_send[...]
    sums = jnp.sum(dp_recv[...], axis=0)
    full = width * dps
    inverse = 1.0 / jnp.sqrt(sums[0:1] / full + epsilon)
    mean = sums[1:2] * inverse / full
    inverse_column = columns(inverse)
    mean_column = columns(mean)
    for h in range(heads):
        span = slice(h * dim, (h + 1) * dim)
        upstream = go_ref[:, span].astype(f32)
        normed = in_buf[h] * inverse_column
        scaled = gain_ref[:, span] * upstream
        d_low = ((scaled - normed * mean_column) * inverse_column).astype(bf16)
        d_buf[h] = d_low
        state[1, h, 0:dim] = mm(qs_buf[h], d_low, TN)
        state[1, h, dim : dim + 1] = jnp.sum(normed * upstream, axis=0, keepdims=True)
        give_head(1, h)

    def inner_backward():
        for h in range(heads):
            span = slice(h * dim, (h + 1) * dim)
            d_low = d_buf[h]
            grad_probs = (mm(d_low, v_ref[:, span], NT) * w_buf[h]).astype(bf16)
            out_scaled = (d_low.astype(f32) * growth_buf[h]).astype(bf16)
            gq = mm(grad_probs, k_ref[:, span], NN) + mm(out_scaled, s_low[h], NT)
            gq_ref[:, span] = gq.astype(bf16)
            gk_part[h] = mm(grad_probs, q_ref[:, span], TN)
            gv_part[h] = mm(p_buf[h], d_low, TN)

    scan(1, inner_backward)
    for h in range(heads):
        r_low[h] = member_recv[1, h, 0:dim].astype(bf16)
        gg_ref[:, h * dim : (h + 1) * dim] = member_recv[1, h, dim : dim + 1]

    for turn in range(2):
        whole_group(turn).wait_send()
        whole_all(turn).wait_send()
        if slices > 1:
            whole_back(turn).wait_send()
        whole_members(turn).wait_send()
    if dps > 1:
        whole_row().wait_send()


def output_kernel(
    gq_in, gk_part, gv_part, vs_ref, ks_ref, r_low, gg_in,
    gq_ref, gk_ref, gv_ref, gg_ref,
    gk_buf, gv_buf, sem,
):
    heads, positions, dim = gk_part.shape
    copies = [
        pltpu.make_async_copy(gq_in, gq_ref, sem.at[0]),
        pltpu.make_async_copy(gg_in, gg_ref, sem.at[1]),
    ]
    for c in copies:
        c.start()
    for h in range(heads):
        span = slice(h * dim, (h + 1) * dim)
        gk = gk_part[h] + mm(vs_ref[h], r_low[h], NT)
        gk_buf[:, span] = gk.astype(bf16)
    copies.append(pltpu.make_async_copy(gk_buf, gk_ref, sem.at[2]))
    copies[-1].start()
    for h in range(heads):
        span = slice(h * dim, (h + 1) * dim)
        gv = gv_part[h] + mm(ks_ref[h], r_low[h], NN)
        gv_buf[:, span] = gv.astype(bf16)
    copies.append(pltpu.make_async_copy(gv_buf, gv_ref, sem.at[3]))
    copies[-1].start()
    for c in copies:
        c.wait()


def local(queries, key_vectors, values, log_decay, norm_gain, grad_out):
    positions, width = queries.shape
    heads = log_decay.shape[0]
    dim = width // heads
    seq = lax.axis_size("seq")
    dps = lax.axis_size("dp")
    groups = seq // heads
    slices = groups // 2
    slab = dim // slices
    padded = dim + 8
    in_hbm = functools.partial(pltpu.with_memory_space_constraint, memory_space=pltpu.HBM)
    vmem = pl.BlockSpec(memory_space=pltpu.VMEM)
    hbm = pl.BlockSpec(memory_space=pltpu.HBM)
    shape = jax.ShapeDtypeStruct
    grad = shape((positions, width), bf16)
    gain_row = shape((1, width), f32)
    middle = (
        grad,
        shape((heads, positions, dim), f32),
        shape((heads, positions, dim), f32),
        shape((heads, positions, dim), bf16),
        shape((heads, positions, dim), bf16),
        shape((heads, dim, dim), bf16),
        gain_row,
    )
    scratch = [
        pltpu.VMEM((positions, width), bf16),
        pltpu.VMEM((positions, width), bf16),
        pltpu.VMEM((positions, width), bf16),
        pltpu.VMEM((heads, positions), f32),
        pltpu.VMEM((1, width), f32),
        pltpu.VMEM((positions, width), bf16),
        pltpu.SemaphoreType.DMA((6,)),
        pltpu.VMEM((heads, positions, positions), f32),
        pltpu.VMEM((heads, positions, positions), bf16),
        pltpu.VMEM((heads, positions, dim), bf16),
        pltpu.VMEM((heads, positions, dim), f32),
        pltpu.VMEM((heads, positions, dim), bf16),
        pltpu.VMEM((heads, dim, dim), bf16),
        pltpu.VMEM((heads, positions, dim), f32),
        pltpu.VMEM((2, positions), f32),
        pltpu.VMEM((dps, 2, positions), f32),
        pltpu.VMEM((2, heads, padded, dim), f32),
        pltpu.VMEM((2, heads, padded, dim), f32),
        pltpu.VMEM((2, slices, slab + 1, dim), f32),
        pltpu.VMEM((2, groups, slab + 1, dim), f32),
        pltpu.VMEM((2, groups, slab, dim), f32),
        pltpu.VMEM((2, slices, slab, dim), f32),
        pltpu.VMEM((2, heads, padded, dim), f32),
        pltpu.VMEM((2, heads, padded, dim), f32),
        pltpu.SemaphoreType.DMA((9,)),
        pltpu.SemaphoreType.DMA((9,)),
    ]
    between = pl.pallas_call(
        exchange_kernel,
        out_shape=middle,
        in_specs=[hbm] * 6,
        out_specs=(vmem,) * len(middle),
        scratch_shapes=scratch,
        compiler_params=pltpu.CompilerParams(
            collective_id=0, has_side_effects=True, vmem_limit_bytes=24 * 1024 * 1024
        ),
    )(*map(in_hbm, (queries, key_vectors, values, log_decay, norm_gain.reshape(1, width), grad_out)))
    gq, gk, gv, gg = pl.pallas_call(
        output_kernel,
        out_shape=(grad, grad, grad, gain_row),
        in_specs=[vmem] * len(middle),
        out_specs=(hbm,) * 4,
        scratch_shapes=[
            pltpu.VMEM((positions, width), bf16),
            pltpu.VMEM((positions, width), bf16),
            pltpu.SemaphoreType.DMA((4,)),
        ],
        compiler_params=pltpu.CompilerParams(vmem_limit_bytes=16 * 1024 * 1024),
    )(*between)
    return gq, gk, gv, gg.reshape(width)


def solution(mesh):
    in_specs = (
        P("seq", "dp"),
        P("seq", "dp"),
        P("seq", "dp"),
        P("dp", "seq"),
        P("dp"),
        P("seq", "dp"),
    )
    out_specs = (P("seq", "dp"), P("seq", "dp"), P("seq", "dp"), P("dp"))
    return jax.shard_map(local, mesh=mesh, in_specs=in_specs, out_specs=out_specs, check_vma=False)
```

time: 122 us -> 103 us (0.84)
  Pallas kernels: 113 us -> 102 us
  local copies, waits for them, and re-layouts: 7.85 us -> 0 us
    pallas_call x1 -> x2, Pallas kernels: 113 us -> 102 us  [the longest x1 101 us: local(): pl.pallas_call(exchange_kernel, out_shape=middle, in_specs=[hbm] * 6, out...]
    unnamed x16 -> x0, local copies, waits for them, and re-layouts: 7.85 us -> none
where the time goes in v2:
time: 103 us
  Pallas kernels  102 us (99%)
    pallas_call x1, Pallas kernels, local(): pl.pallas_call(exchange_kernel, out_shape=middle, in_specs=[hbm] * 6, out...  101 us

profile of v2, /device:TPU:1, one launch (start us, length us, event | category | flops | bytes accessed | tf_op | source)
XLA Modules:
  0.0 102.6 jit_solution(14288338815893410314)
XLA Ops:
  0.6 100.9 %shard_map.93 = (bf16[256,512]{1,0:T(8,128)(2,1)S(1)}, f32[4,256,128]{2,1,0:T(8,128)S(1)}, f32[4,256,128]{2,1,0:T(8,128)S(1)}, bf16[4,256,128]{2,1,0:T(8,128)(2,...) custom-call(bf16[256,512]{1,0:T(8,128)(2,1)} %q_hbm.1, ...), custom_call_target="tpu_custom_call" | custom-call | tf_op jit(solution)/shard_map/pallas_call | solution.py:417
  101.6 1.1 %shard_map.94 = (bf16[256,512]{1,0:T(8,128)(2,1)}, bf16[256,512]{1,0:T(8,128)(2,1)}, bf16[256,512]{1,0:T(8,128)(2,1)}, f32[1,512]{1,0:T(1,128)}) custom-call(bf16[256,512]{1,0:T(8,128)(2,1)S(1)} %get-tuple-element.15.gq_in, f32[4,256,128]{2,1,0:T(8,128)S(1)} %get-tuple-element.16.gk_part, f32[4,256,128]{2,1,0:T(8,128)S(1)} %get-tuple-element.17.gv_part, ...), custom_call_target="tpu_custom_call" | custom-call | tf_op jit(solution)/shard_map/pallas_call | solution.py:427

commit v3 on v2

--- a/solution.py
+++ b/solution.py
@@ -16,7 +16,7 @@
 NT = (((1,), (1,)), ((), ()))
 TN = (((0,), (0,)), ((), ()))
 
-GROUP, ALL, BACK, MEMBERS, ROW = 0, 1, 2, 3, 8
+GROUP, ALL, BACK, MEMBERS, ROW, GAIN = 0, 1, 2, 3, 8, 9
 
 
 def mm(a, b, dims):
@@ -30,7 +30,8 @@
     w_buf, p_buf, qs_buf, in_buf, d_buf, s_low, growth_buf,
     dp_send, dp_recv,
     state, part, all_send, all_recv, back_send, back_recv, member_send, member_recv,
-    send_sem, recv_sem,
+    gain_own, gain_rows,
+    send_sem, recv_sem, slice_sem, hello,
 ):
     seq = lax.axis_size("seq")
     dps = lax.axis_size("dp")
@@ -74,15 +75,20 @@
     def greet(target):
         pl.semaphore_signal(barrier, inc=1, device_id=target, device_id_type=MESH)
 
-    def greet_all(step, carry):
-        greet({"seq": in_all(step)})
+    def rank_of(which):
+        return jnp.where(which < slices, which, 3 * slices - 1 - which)
+
+    rank = rank_of(group)
+
+    def greet_all(place_in_wave, carry):
+        greet({"seq": rank_of(place_in_wave) * heads + member})
         return carry
 
     def greet_row(step, carry):
         greet({"dp": lax.rem(row + step, dps)})
         return carry
 
-    lax.fori_loop(1, groups, greet_all, 0)
+    lax.fori_loop(rank + 1, groups, greet_all, 0)
     lax.fori_loop(1, dps, greet_row, 0)
     for step in range(1, heads):
         greet({"seq": in_group(step)})
@@ -114,33 +120,45 @@
         state[0, h, 0:dim] = mm(key_scaled, v, TN)
         state[0, h, dim : dim + 1] = jnp.broadcast_to(jnp.exp(last), (1, dim))
 
-    loads[3].wait()
-    causal = lax.broadcasted_iota(
-        jnp.int32, (positions, positions), 0
-    ) >= lax.broadcasted_iota(jnp.int32, (positions, positions), 1)
-    for h in range(heads):
-        span = slice(h * dim, (h + 1) * dim)
-        line = run[h : h + 1]
-        wide = jnp.concatenate([columns(line)] * (positions // dim), axis=1)
-        spread = jnp.where(causal, wide - line, 0.0)
-        weights = jnp.where(causal, jnp.exp(spread), 0.0)
-        w_buf[h] = weights
-        q = q_ref[:, span]
-        probs = (mm(q, k_ref[:, span], NT) * weights).astype(bf16)
-        p_buf[h] = probs
-        qs_buf[h] = (q.astype(f32) * growth_buf[h]).astype(bf16)
-        in_buf[h] = mm(probs, v_ref[:, span], NN)
-    loads[4].wait()
-    loads[5].wait()
-
-    pl.semaphore_wait(barrier, groups - 1 + dps - 1 + heads - 1)
-
-    def copy(src, dst, index, target):
+    def inner_forward():
+        loads[3].wait()
+        causal = lax.broadcasted_iota(
+            jnp.int32, (positions, positions), 0
+        ) >= lax.broadcasted_iota(jnp.int32, (positions, positions), 1)
+        for h in range(heads):
+            span = slice(h * dim, (h + 1) * dim)
+            line = run[h : h + 1]
+            wide = jnp.concatenate([columns(line)] * (positions // dim), axis=1)
+            spread = jnp.where(causal, wide - line, 0.0)
+            weights = jnp.where(causal, jnp.exp(spread), 0.0)
+            w_buf[h] = weights
+            q = q_ref[:, span]
+            probs = (mm(q, k_ref[:, span], NT) * weights).astype(bf16)
+            p_buf[h] = probs
+            qs_buf[h] = (q.astype(f32) * growth_buf[h]).astype(bf16)
+            in_buf[h] = mm(probs, v_ref[:, span], NN)
+        loads[4].wait()
+        loads[5].wait()
+
+    pl.semaphore_wait(barrier, rank + dps - 1 + heads - 1)
+
+    def greet_back(place_in_wave, carry):
+        pl.semaphore_signal(
+            hello.at[group],
+            inc=1,
+            device_id={"seq": rank_of(place_in_wave) * heads + member},
+            device_id_type=MESH,
+        )
+        return carry
+
+    lax.fori_loop(0, rank, greet_back, 0)
+
+    def copy(src, dst, index, target, arrived=None):
         return pltpu.make_async_remote_copy(
             src_ref=src,
             dst_ref=dst,
             send_sem=send_sem.at[index],
-            recv_sem=recv_sem.at[index],
+            recv_sem=recv_sem.at[index] if arrived is None else arrived,
             device_id=target,
             device_id_type=MESH,
         )
@@ -172,9 +190,12 @@
         return copy(box, box, turn * 4 + BACK, neighbour)
 
     def whole_members(turn):
-        rows = dim + turn
-        box = member_recv.at[turn, pl.ds(0, heads - 1), pl.ds(0, rows)]
+        box = member_recv.at[turn, pl.ds(0, heads - 1)]
         return copy(box, box, turn * 4 + MEMBERS, neighbour)
+
+    def whole_gain():
+        box = gain_rows.at[pl.ds(0, heads - 1)]
+        return copy(box, box, GAIN, neighbour)
 
     def whole_row():
         box = dp_recv.at[pl.ds(0, dps - 1)]
@@ -201,8 +222,7 @@
             all_send[turn, s, 0:slab] = total[s * slab : (s + 1) * slab]
             all_send[turn, s, slab : slab + 1] = tail
 
-        def give(step):
-            target = lax.rem(group + step, groups)
+        def give(target):
             copy(
                 all_send.at[turn, lax.rem(target, slices)],
                 all_recv.at[turn, group],
@@ -210,14 +230,29 @@
                 {"seq": target * heads + member},
             ).start()
 
-        give(slices)
-
-        def both(t, carry):
-            give(slices - t)
-            give(slices + t)
+        def in_wave(place_in_wave, carry):
+            target = rank_of(place_in_wave)
+
+            @pl.when(place_in_wave > rank)
+            def _():
+                pl.semaphore_wait(hello.at[target], 1)
+
+            @pl.when(place_in_wave != rank)
+            def _():
+                give(target)
+
             return carry
 
-        lax.fori_loop(1, slices, both, 0)
+        def far_first(t, carry):
+            give(lax.rem(group + slices - t, groups))
+            give(lax.rem(group + slices + t, groups))
+            return carry
+
+        if turn == 0:
+            lax.fori_loop(0, groups, in_wave, 0)
+        else:
+            give(lax.rem(group + slices, groups))
+            lax.fori_loop(1, slices, far_first, 0)
         fill()
         whole_all(turn).wait_recv()
         all_recv[turn, group] = all_send[turn, lax.rem(group, slices)]
@@ -233,6 +268,7 @@
                 back_recv.at[turn, lax.rem(group, slices)],
                 turn * 4 + BACK,
                 {"seq": target * heads + member},
+                slice_sem.at[turn, step + behind],
             ).start()
 
         for t in range(ahead, 0, -1):
@@ -243,36 +279,50 @@
             gain_total = all_recv[1, 0, slab : slab + 1]
             for i in range(1, groups):
                 gain_total = gain_total + all_recv[1, i, slab : slab + 1]
-        if slices > 1:
-            whole_back(turn).wait_recv()
-        back_recv[turn, lax.rem(group, slices)] = back_send[turn, group]
-        entering = back_recv[turn].reshape(dim, dim)
-        for i in order:
-            member_send[turn, i, 0:dim] = entering
-            entering = decay[i] * entering + part[turn, i, 0:dim]
-            if turn == 1:
-                member_send[turn, i, dim : dim + 1] = gain_total
-        rows = pl.ds(0, dim + turn)
-        for t in (2, 1, 3) if heads == 4 else range(1, heads):
-            target = lax.rem(member + t, heads)
-            copy(
-                member_send.at[turn, target, rows],
-                member_recv.at[turn, member, rows],
-                turn * 4 + MEMBERS,
-                {"seq": group * heads + target},
-            ).start()
+            gain_own[...] = gain_total
+            for t in range(1, heads):
+                copy(gain_own, gain_rows.at[member], GAIN, {"seq": in_group(t)}).start()
+
+        def pass_on(step):
+            which = lax.rem(group + groups - step, slices)
+            rows = pl.ds(pl.multiple_of(which * slab, slab), slab)
+            if step == 0:
+                entering = back_send[turn, group]
+            else:
+                box = back_recv.at[turn, which]
+                copy(
+                    box, box, turn * 4 + BACK, neighbour, slice_sem.at[turn, step + behind]
+                ).wait_recv()
+                entering = back_recv[turn, which]
+            for i in order:
+                member_send[turn, i, rows] = entering
+                entering = decay[i] * entering + part[turn, i, rows]
+            for t in (2, 1, 3) if heads == 4 else range(1, heads):
+                target = lax.rem(member + t, heads)
+                copy(
+                    member_send.at[turn, target, rows],
+                    member_recv.at[turn, member, rows],
+                    turn * 4 + MEMBERS,
+                    {"seq": group * heads + target},
+                ).start()
+
+        pass_on(0)
+        for t in range(1, ahead + 1):
+            if t <= behind:
+                pass_on(-t)
+            pass_on(t)
         whole_members(turn).wait_recv()
         member_recv[turn, member] = member_send[turn, member]
 
     for h in range(heads):
         give_head(0, h)
-    scan(0, lambda: None)
+    scan(0, inner_forward)
 
     squares = jnp.zeros((positions, dim), f32)
     products = jnp.zeros((positions, dim), f32)
     for h in range(heads):
         span = slice(h * dim, (h + 1) * dim)
-        low = member_recv[0, h, 0:dim].astype(bf16)
+        low = member_recv[0, h].astype(bf16)
         s_low[h] = low
         attended = in_buf[h] + mm(qs_buf[h], low, NN)
         in_buf[h] = attended
@@ -320,8 +370,11 @@
 
     scan(1, inner_backward)
     for h in range(heads):
-        r_low[h] = member_recv[1, h, 0:dim].astype(bf16)
-        gg_ref[:, h * dim : (h + 1) * dim] = member_recv[1, h, dim : dim + 1]
+        r_low[h] = member_recv[1, h].astype(bf16)
+    whole_gain().wait_recv()
+    gain_rows[member] = gain_own[...]
+    for h in range(heads):
+        gg_ref[:, h * dim : (h + 1) * dim] = gain_rows[h]
 
     for turn in range(2):
         whole_group(turn).wait_send()
@@ -329,6 +382,7 @@
         if slices > 1:
             whole_back(turn).wait_send()
         whole_members(turn).wait_send()
+    whole_gain().wait_send()
     if dps > 1:
         whole_row().wait_send()
 
@@ -409,10 +463,14 @@
         pltpu.VMEM((2, groups, slab + 1, dim), f32),
         pltpu.VMEM((2, groups, slab, dim), f32),
         pltpu.VMEM((2, slices, slab, dim), f32),
-        pltpu.VMEM((2, heads, padded, dim), f32),
-        pltpu.VMEM((2, heads, padded, dim), f32),
-        pltpu.SemaphoreType.DMA((9,)),
-        pltpu.SemaphoreType.DMA((9,)),
+        pltpu.VMEM((2, heads, dim, dim), f32),
+        pltpu.VMEM((2, heads, dim, dim), f32),
+        pltpu.VMEM((1, dim), f32),
+        pltpu.VMEM((heads, 1, dim), f32),
+        pltpu.SemaphoreType.DMA((10,)),
+        pltpu.SemaphoreType.DMA((10,)),
+        pltpu.SemaphoreType.DMA((2, slices)),
+        pltpu.SemaphoreType.REGULAR((groups,)),
     ]
     between = pl.pallas_call(
         exchange_kernel,

time: 103 us -> 111 us (1.078)
  Pallas kernels: 102 us -> 110 us
    pallas_call x1, Pallas kernels: 101 us -> 109 us  [local(): pl.pallas_call(exchange_kernel, out_shape=middle, in_specs=[hbm] * 6, out...]
where the time goes in v3:
time: 111 us; the launch traced here: 110 us
  Pallas kernels  110 us (99%)
    pallas_call x1, Pallas kernels, local(): pl.pallas_call(exchange_kernel, out_shape=middle, in_specs=[hbm] * 6, out...  109 us

profile of v3, /device:TPU:1, one launch (start us, length us, event | category | flops | bytes accessed | tf_op | source)
XLA Modules:
  0.0 110.4 jit_solution(13165480200756006939)
XLA Ops:
  0.6 108.7 %shard_map.93 = (bf16[256,512]{1,0:T(8,128)(2,1)S(1)}, f32[4,256,128]{2,1,0:T(8,128)S(1)}, f32[4,256,128]{2,1,0:T(8,128)S(1)}, bf16[4,256,128]{2,1,0:T(8,128)(2,...) custom-call(bf16[256,512]{1,0:T(8,128)(2,1)} %q_hbm.1, ...), custom_call_target="tpu_custom_call" | custom-call | tf_op jit(solution)/shard_map/pallas_call | solution.py:475
  109.4 1.1 shard_map.94

commit v4 on v3

--- a/solution.py
+++ b/solution.py
@@ -31,7 +31,7 @@
     dp_send, dp_recv,
     state, part, all_send, all_recv, back_send, back_recv, member_send, member_recv,
     gain_own, gain_rows,
-    send_sem, recv_sem, slice_sem, hello,
+    send_sem, recv_sem, slice_sem,
 ):
     seq = lax.axis_size("seq")
     dps = lax.axis_size("dp")
@@ -75,20 +75,15 @@
     def greet(target):
         pl.semaphore_signal(barrier, inc=1, device_id=target, device_id_type=MESH)
 
-    def rank_of(which):
-        return jnp.where(which < slices, which, 3 * slices - 1 - which)
-
-    rank = rank_of(group)
-
-    def greet_all(place_in_wave, carry):
-        greet({"seq": rank_of(place_in_wave) * heads + member})
+    def greet_all(step, carry):
+        greet({"seq": in_all(step)})
         return carry
 
     def greet_row(step, carry):
         greet({"dp": lax.rem(row + step, dps)})
         return carry
 
-    lax.fori_loop(rank + 1, groups, greet_all, 0)
+    lax.fori_loop(1, groups, greet_all, 0)
     lax.fori_loop(1, dps, greet_row, 0)
     for step in range(1, heads):
         greet({"seq": in_group(step)})
@@ -140,18 +135,7 @@
         loads[4].wait()
         loads[5].wait()
 
-    pl.semaphore_wait(barrier, rank + dps - 1 + heads - 1)
-
-    def greet_back(place_in_wave, carry):
-        pl.semaphore_signal(
-            hello.at[group],
-            inc=1,
-            device_id={"seq": rank_of(place_in_wave) * heads + member},
-            device_id_type=MESH,
-        )
-        return carry
-
-    lax.fori_loop(0, rank, greet_back, 0)
+    pl.semaphore_wait(barrier, groups - 1 + dps - 1 + heads - 1)
 
     def copy(src, dst, index, target, arrived=None):
         return pltpu.make_async_remote_copy(
@@ -230,29 +214,13 @@
                 {"seq": target * heads + member},
             ).start()
 
-        def in_wave(place_in_wave, carry):
-            target = rank_of(place_in_wave)
-
-            @pl.when(place_in_wave > rank)
-            def _():
-                pl.semaphore_wait(hello.at[target], 1)
-
-            @pl.when(place_in_wave != rank)
-            def _():
-                give(target)
-
-            return carry
-
         def far_first(t, carry):
             give(lax.rem(group + slices - t, groups))
             give(lax.rem(group + slices + t, groups))
             return carry
 
-        if turn == 0:
-            lax.fori_loop(0, groups, in_wave, 0)
-        else:
-            give(lax.rem(group + slices, groups))
-            lax.fori_loop(1, slices, far_first, 0)
+        give(lax.rem(group + slices, groups))
+        lax.fori_loop(1, slices, far_first, 0)
         fill()
         whole_all(turn).wait_recv()
         all_recv[turn, group] = all_send[turn, lax.rem(group, slices)]
@@ -470,7 +438,6 @@
         pltpu.SemaphoreType.DMA((10,)),
         pltpu.SemaphoreType.DMA((10,)),
         pltpu.SemaphoreType.DMA((2, slices)),
-        pltpu.SemaphoreType.REGULAR((groups,)),
     ]
     between = pl.pallas_call(
         exchange_kernel,

time: 111 us -> 98.9 us (0.89)
  Pallas kernels: 110 us -> 98.1 us
    pallas_call x1, Pallas kernels: 109 us -> 97 us  [local(): pl.pallas_call(exchange_kernel, out_shape=middle, in_specs=[hbm] * 6, out...]
where the time goes in v4:
time: 98.9 us; the launch traced here: 98.8 us
  Pallas kernels  98.1 us (99%)
    pallas_call x1, Pallas kernels, local(): pl.pallas_call(exchange_kernel, out_shape=middle, in_specs=[hbm] * 6, out...  97 us

profile of v4, /device:TPU:1, one launch (start us, length us, event | category | flops | bytes accessed | tf_op | source)
XLA Modules:
  0.0 98.8 jit_solution(17971344129023720533)
XLA Ops:
  0.6 97.0 %shard_map.93 = (bf16[256,512]{1,0:T(8,128)(2,1)S(1)}, f32[4,256,128]{2,1,0:T(8,128)S(1)}, f32[4,256,128]{2,1,0:T(8,128)S(1)}, bf16[4,256,128]{2,1,0:T(8,128)(2,...) custom-call(bf16[256,512]{1,0:T(8,128)(2,1)} %q_hbm.1, ...), custom_call_target="tpu_custom_call" | custom-call | tf_op jit(solution)/shard_map/pallas_call | solution.py:442
  97.7 1.1 %shard_map.94 = (bf16[256,512]{1,0:T(8,128)(2,1)}, bf16[256,512]{1,0:T(8,128)(2,1)}, bf16[256,512]{1,0:T(8,128)(2,1)}, f32[1,512]{1,0:T(1,128)}) custom-call(bf16[256,512]{1,0:T(8,128)(2,1)S(1)} %get-tuple-element.15.gq_in, f32[4,256,128]{2,1,0:T(8,128)S(1)} %get-tuple-element.16.gk_part, f32[4,256,128]{2,1,0:T(8,128)S(1)} %get-tuple-element.17.gv_part, ...), custom_call_target="tpu_custom_call" | custom-call | tf_op jit(solution)/shard_map/pallas_call | solution.py:452

commit v5 on v4

--- a/solution.py
+++ b/solution.py
@@ -30,7 +30,7 @@
     w_buf, p_buf, qs_buf, in_buf, d_buf, s_low, growth_buf,
     dp_send, dp_recv,
     state, part, all_send, all_recv, back_send, back_recv, member_send, member_recv,
-    gain_own, gain_rows,
+    gain_own, gain_rows, gain_part, gain_groups,
     send_sem, recv_sem, slice_sem,
 ):
     seq = lax.axis_size("seq")
@@ -67,8 +67,16 @@
     def in_group(step):
         return group * heads + lax.rem(member + step, heads)
 
+    def keeper(which, h):
+        return lax.rem(h + lax.div(which, slices) * (heads // 2), heads)
+
+    head = keeper(group, member)
+
+    def holder(which):
+        return which * heads + keeper(which, head)
+
     def in_all(step):
-        return lax.rem(group + step, groups) * heads + member
+        return holder(lax.rem(group + step, groups))
 
     barrier = pltpu.get_barrier_semaphore()
 
@@ -152,13 +160,13 @@
     def give_head(turn, h):
         rows = pl.ds(0, dim + 1)
 
-        @pl.when(h != member)
+        @pl.when(h != head)
         def _():
             copy(
                 state.at[turn, h, rows],
                 part.at[turn, member, rows],
                 turn * 4 + GROUP,
-                {"seq": group * heads + h},
+                {"seq": group * heads + keeper(group, h)},
             ).start()
 
     def whole_group(turn):
@@ -166,7 +174,7 @@
         return copy(box, box, turn * 4 + GROUP, neighbour)
 
     def whole_all(turn):
-        box = all_recv.at[turn, pl.ds(0, groups - 1)]
+        box = all_recv.at[turn, pl.ds(0, groups - 1), pl.ds(0, slab + 1 - turn)]
         return copy(box, box, turn * 4 + ALL, neighbour)
 
     def whole_back(turn):
@@ -188,7 +196,7 @@
     def scan(turn, fill):
         order = range(heads) if turn == 0 else range(heads - 1, -1, -1)
         whole_group(turn).wait_recv()
-        part[turn, member] = state[turn, member]
+        part[turn, member] = state[turn, head]
         decay = [part[0, i, dim : dim + 1] for i in range(heads)]
         total = None
         for i in order:
@@ -207,11 +215,12 @@
             all_send[turn, s, slab : slab + 1] = tail
 
         def give(target):
+            rows = pl.ds(0, slab + 1 - turn)
             copy(
-                all_send.at[turn, lax.rem(target, slices)],
-                all_recv.at[turn, group],
+                all_send.at[turn, lax.rem(target, slices), rows],
+                all_recv.at[turn, group, rows],
                 turn * 4 + ALL,
-                {"seq": target * heads + member},
+                {"seq": holder(target)},
             ).start()
 
         def far_first(t, carry):
@@ -221,6 +230,16 @@
 
         give(lax.rem(group + slices, groups))
         lax.fori_loop(1, slices, far_first, 0)
+        if turn == 1:
+            gain_part[...] = tail
+
+            def give_gain(t, carry):
+                copy(
+                    gain_part, gain_groups.at[group], GAIN + 1, {"seq": in_all(t)}
+                ).start()
+                return carry
+
+            lax.fori_loop(1, groups, give_gain, 0)
         fill()
         whole_all(turn).wait_recv()
         all_recv[turn, group] = all_send[turn, lax.rem(group, slices)]
@@ -235,7 +254,7 @@
                 back_send.at[turn, target],
                 back_recv.at[turn, lax.rem(group, slices)],
                 turn * 4 + BACK,
-                {"seq": target * heads + member},
+                {"seq": holder(target)},
                 slice_sem.at[turn, step + behind],
             ).start()
 
@@ -243,13 +262,6 @@
             give_back(t)
             if t <= behind:
                 give_back(-t)
-        if turn == 1:
-            gain_total = all_recv[1, 0, slab : slab + 1]
-            for i in range(1, groups):
-                gain_total = gain_total + all_recv[1, i, slab : slab + 1]
-            gain_own[...] = gain_total
-            for t in range(1, heads):
-                copy(gain_own, gain_rows.at[member], GAIN, {"seq": in_group(t)}).start()
 
         def pass_on(step):
             which = lax.rem(group + groups - step, slices)
@@ -269,7 +281,7 @@
                 target = lax.rem(member + t, heads)
                 copy(
                     member_send.at[turn, target, rows],
-                    member_recv.at[turn, member, rows],
+                    member_recv.at[turn, head, rows],
                     turn * 4 + MEMBERS,
                     {"seq": group * heads + target},
                 ).start()
@@ -279,8 +291,15 @@
             if t <= behind:
                 pass_on(-t)
             pass_on(t)
+        if turn == 1:
+            box = gain_groups.at[pl.ds(0, groups - 1)]
+            copy(box, box, GAIN + 1, neighbour).wait()
+            gain_groups[group] = all_send[1, 0, slab : slab + 1]
+            gain_own[...] = jnp.sum(gain_groups[...], axis=0)
+            for t in range(1, heads):
+                copy(gain_own, gain_rows.at[head], GAIN, {"seq": in_group(t)}).start()
         whole_members(turn).wait_recv()
-        member_recv[turn, member] = member_send[turn, member]
+        member_recv[turn, head] = member_send[turn, member]
 
     for h in range(heads):
         give_head(0, h)
@@ -340,7 +359,7 @@
     for h in range(heads):
         r_low[h] = member_recv[1, h].astype(bf16)
     whole_gain().wait_recv()
-    gain_rows[member] = gain_own[...]
+    gain_rows[head] = gain_own[...]
     for h in range(heads):
         gg_ref[:, h * dim : (h + 1) * dim] = gain_rows[h]
 
@@ -435,8 +454,10 @@
         pltpu.VMEM((2, heads, dim, dim), f32),
         pltpu.VMEM((1, dim), f32),
         pltpu.VMEM((heads, 1, dim), f32),
-        pltpu.SemaphoreType.DMA((10,)),
-        pltpu.SemaphoreType.DMA((10,)),
+        pltpu.VMEM((1, dim), f32),
+        pltpu.VMEM((groups, 1, dim), f32),
+        pltpu.SemaphoreType.DMA((11,)),
+        pltpu.SemaphoreType.DMA((11,)),
         pltpu.SemaphoreType.DMA((2, slices)),
     ]
     between = pl.pallas_call(

time: 98.9 us -> 98.1 us (level)
  no operation moved by 1% of the time
where the time goes in v5:
time: 98.1 us; the launch traced here: 98 us
  Pallas kernels  97.4 us (99%)
    pallas_call x1, Pallas kernels, local(): pl.pallas_call(exchange_kernel, out_shape=middle, in_specs=[hbm] * 6, out...  96.3 us

profile of v5, /device:TPU:1, one launch (start us, length us, event | category | flops | bytes accessed | tf_op | source)
XLA Modules:
  0.0 98.0 jit_solution(3812549734989791814)
XLA Ops:
  0.6 96.3 %shard_map.93 = (bf16[256,512]{1,0:T(8,128)(2,1)S(1)}, f32[4,256,128]{2,1,0:T(8,128)S(1)}, f32[4,256,128]{2,1,0:T(8,128)S(1)}, bf16[4,256,128]{2,1,0:T(8,128)(2,...) custom-call(bf16[256,512]{1,0:T(8,128)(2,1)} %q_hbm.1, ...), custom_call_target="tpu_custom_call" | custom-call | tf_op jit(solution)/shard_map/pallas_call | solution.py:463
  96.9 1.1 %shard_map.94 = (bf16[256,512]{1,0:T(8,128)(2,1)}, bf16[256,512]{1,0:T(8,128)(2,1)}, bf16[256,512]{1,0:T(8,128)(2,1)}, f32[1,512]{1,0:T(1,128)}) custom-call(bf16[256,512]{1,0:T(8,128)(2,1)S(1)} %get-tuple-element.15.gq_in, f32[4,256,128]{2,1,0:T(8,128)S(1)} %get-tuple-element.16.gk_part, f32[4,256,128]{2,1,0:T(8,128)S(1)} %get-tuple-element.17.gv_part, ...), custom_call_target="tpu_custom_call" | custom-call | tf_op jit(solution)/shard_map/pallas_call | solution.py:473
